TPU v7x, 32 devices: a whole 2x2x4 slice. The times are simulated.
32 devices in a mesh: gx: 2 (over x), gy: 4 (over y, core), gz: 4 (over z).
Axes of the slice: x: 2, y: 2, z: 4, core: 2. Of those that a mesh axis runs over, the one named last changes fastest.
Arguments:
- node_feat: bfloat16 [16, 32, 32, 128], P('gx', 'gy', 'gz'), may hold values from -6 to 6
- edge_feat: bfloat16 [4, 16, 32, 32, 128], P(None, 'gx', 'gy', 'gz'), may hold values from -6 to 6
- copies: int32 [16, 32, 32], P('gx', 'gy', 'gz'), may hold values from 1 to 8
- offsets: int32 [4, 3], replicated, may hold values from -1 to 1
- w_edge_in: bfloat16 [384, 128], replicated, may hold values from -0.3125 to 0.3125
- w_edge_out: bfloat16 [128, 128], replicated, may hold values from -0.5 to 0.5
- w_node_in: bfloat16 [256, 128], replicated, may hold values from -0.375 to 0.375
- w_node_out: bfloat16 [128, 128], replicated, may hold values from -0.5 to 0.5
- node_cot: bfloat16 [16, 32, 32, 128], P('gx', 'gy', 'gz'), may hold values from -6 to 6
Outputs:
- node_grad: bfloat16 [16, 32, 32, 128], P('gx', 'gy', 'gz')
- edge_grad: bfloat16 [4, 16, 32, 32, 128], P(None, 'gx', 'gy', 'gz')
- grad_edge_in: float32 [384, 128], replicated
- grad_edge_out: float32 [128, 128], replicated
- grad_node_in: float32 [256, 128], replicated
- grad_node_out: float32 [128, 128], replicated
Inputs may be any that keep to these rules, and one draw needn't show every extreme that they name: `offsets`: each row is one lattice offset, its three entries along the first, second and third dimension.
All inputs are finite; a program needn't handle non-finite values.
Results may differ from a plain program's by a relative error of at most 0.0068.
Values sent between devices are 32-bit elements; how exact they have to be, the bound alone decides.
A program may use at most 64 MiB of HBM per device.

v0:
```python
import math

import jax
import jax.numpy as jnp
from jax import lax
from jax.sharding import PartitionSpec as P


def extended(block, sides, width):
    for axis, dim in sides:
        count = lax.axis_size(axis)
        forward = [(i, i + 1) for i in range(count - 1)]
        backward = [(target, source) for source, target in forward]
        low = lax.ppermute(
            lax.slice_in_dim(block, block.shape[dim] - width, None, axis=dim), axis, forward
        )
        high = lax.ppermute(lax.slice_in_dim(block, 0, width, axis=dim), axis, backward)
        block = jnp.concatenate([low, block, high], axis=dim)
    return block


def neighbour_valid(offset, brick):
    coords = jnp.arange(brick, dtype=jnp.int32)
    inside = [
        (coords + offset[which] >= 0) & (coords + offset[which] < brick) for which in range(3)
    ]
    joined = inside[0][:, None, None] & inside[1][None, :, None] & inside[2][None, None, :]
    return joined.astype(jnp.float32).reshape(brick * brick * brick, 1)


def moved_view(field, corner):
    padded = jnp.pad(field, ((1, 1), (1, 1), (1, 1), (0, 0)))
    start = 1 + corner
    return lax.dynamic_slice(padded, (start[0], start[1], start[2], jnp.int32(0)), field.shape)


def silu_slope(preact):
    sigma = jax.nn.sigmoid(preact)
    return sigma * (1.0 + preact * (1.0 - sigma))


def outer_product(left, right):
    return lax.dot_general(
        left, right, (((0,), (0,)), ((), ())), preferred_element_type=jnp.float32
    )


def edge_preact(sender, receiver, feature, w_edge_in, width):
    total = jnp.dot(sender, w_edge_in[:width], preferred_element_type=jnp.float32)
    total = total + jnp.dot(
        receiver, w_edge_in[width : 2 * width], preferred_element_type=jnp.float32
    )
    return total + jnp.dot(feature, w_edge_in[2 * width :], preferred_element_type=jnp.float32)


def edge_messages(nodes, edges, offsets, w_edge_in, w_edge_out):
    brick = nodes.shape[0]
    width = nodes.shape[3]
    count = brick * brick * brick
    receiver = nodes.reshape(count, width)
    total = jnp.zeros((count, width), jnp.float32)
    preacts = []
    hiddens = []
    for kind_index in range(edges.shape[0]):
        offset = offsets[kind_index]
        sender = moved_view(nodes, offset).reshape(count, width)
        preact = edge_preact(
            sender, receiver, edges[kind_index].reshape(count, width), w_edge_in, width
        )
        hidden = jax.nn.silu(preact).astype(jnp.bfloat16)
        message = jnp.dot(hidden, w_edge_out, preferred_element_type=jnp.float32)
        total = total + neighbour_valid(offset, brick) * message
        preacts.append(preact)
        hiddens.append(hidden)
    return (total.reshape(nodes.shape), preacts, hiddens)


def node_backward(nodes, summed, copies, node_cot, w_node_in, w_node_out):
    width = nodes.shape[3]
    count = nodes.shape[0] * nodes.shape[1] * nodes.shape[2]
    receiver = nodes.reshape(count, width)
    scale = copies.reshape(count, 1).astype(jnp.float32)
    gathered = (summed.reshape(count, width) / scale).astype(jnp.bfloat16)
    preact = jnp.dot(receiver, w_node_in[:width], preferred_element_type=jnp.float32)
    preact = preact + jnp.dot(gathered, w_node_in[width:], preferred_element_type=jnp.float32)
    hidden = jax.nn.silu(preact).astype(jnp.bfloat16)
    upstream = node_cot.reshape(count, width)
    grad_out = outer_product(hidden, upstream)
    slope = (
        jnp.dot(upstream, w_node_out.T, preferred_element_type=jnp.float32) * silu_slope(preact)
    ).astype(jnp.bfloat16)
    grad_in = jnp.concatenate(
        [outer_product(receiver, slope), outer_product(gathered, slope)], axis=0
    )
    to_nodes = jnp.dot(slope, w_node_in[:width].T, preferred_element_type=jnp.float32)
    to_agg = jnp.dot(slope, w_node_in[width:].T, preferred_element_type=jnp.float32) / scale
    return (to_nodes.reshape(nodes.shape), to_agg.reshape(nodes.shape), grad_in, grad_out)


def edge_backward(nodes, edges, offsets, incoming, w_edge_in, w_edge_out, preacts, hiddens):
    brick = nodes.shape[0]
    width = nodes.shape[3]
    count = brick * brick * brick
    receiver = nodes.reshape(count, width)
    arriving = incoming.reshape(count, width)
    grad_in = jnp.zeros((3 * width, width), jnp.float32)
    grad_out = jnp.zeros((width, width), jnp.float32)
    to_nodes = jnp.zeros((count, width), jnp.float32)
    sent_back = jnp.zeros(nodes.shape, jnp.float32)
    edge_grads = []
    for kind_index in range(edges.shape[0]):
        offset = offsets[kind_index]
        sender = moved_view(nodes, offset).reshape(count, width)
        feature = edges[kind_index].reshape(count, width)
        message_cot = (neighbour_valid(offset, brick) * arriving).astype(jnp.bfloat16)
        grad_out = grad_out + outer_product(hiddens[kind_index], message_cot)
        slope = jnp.dot(message_cot, w_edge_out.T, preferred_element_type=jnp.float32) * silu_slope(
            preacts[kind_index]
        )
        slope = slope.astype(jnp.bfloat16)
        grad_in = grad_in + jnp.concatenate(
            [
                outer_product(sender, slope),
                outer_product(receiver, slope),
                outer_product(feature, slope),
            ],
            axis=0,
        )
        to_nodes = to_nodes + jnp.dot(
            slope, w_edge_in[width : 2 * width].T, preferred_element_type=jnp.float32
        )
        from_sender = jnp.dot(
            slope, w_edge_in[:width].T, preferred_element_type=jnp.float32
        ).reshape(nodes.shape)
        sent_back = sent_back + moved_view(from_sender, -offset)
        edge_grads.append(
            jnp.dot(slope, w_edge_in[2 * width :].T, preferred_element_type=jnp.float32)
            .astype(jnp.bfloat16)
            .reshape(nodes.shape)
        )
    return (to_nodes.reshape(nodes.shape) + sent_back, jnp.stack(edge_grads), grad_in, grad_out)


def clip_all(grads):
    squares = sum((jnp.sum(single * single) for single in grads))
    entries = sum((single.size for single in grads))
    factor = math.sqrt(entries) / jnp.sqrt(squares)
    return tuple((single * factor for single in grads))


def rim_planes(field, which):
    depth = field.shape[which]
    lower = lax.slice_in_dim(field, 0, 1, axis=which)
    upper = lax.slice_in_dim(field, depth - 1, depth, axis=which)
    return (lower, upper)


def joined_rims(field, which, lower, upper, before, after):
    depth = field.shape[which]
    middle = lax.slice_in_dim(field, 1, depth - 1, axis=which)
    return jnp.concatenate([lower + before, middle, upper + after], axis=which)


def fold_rims(padded, which):
    depth = padded.shape[which]
    first = lax.slice_in_dim(padded, 0, 1, axis=which)
    last = lax.slice_in_dim(padded, depth - 1, depth, axis=which)
    inner = lax.slice_in_dim(padded, 1, depth - 1, axis=which)
    lower, upper = rim_planes(inner, which)
    return joined_rims(inner, which, lower, upper, first, last)


def assemble(field):
    padded = extended(field, (("gx", 0), ("gy", 1), ("gz", 2)), 1)
    for which in range(3):
        padded = fold_rims(padded, which)
    return padded


def on_device(
    node_feat, edge_feat, copies, offsets, w_edge_in, w_edge_out, w_node_in, w_node_out, node_cot
):
    local_sum, preacts, hiddens = edge_messages(
        node_feat, edge_feat, offsets, w_edge_in, w_edge_out
    )
    summed = assemble(local_sum)
    node_part, agg_part, node_in_grad, node_out_grad = node_backward(
        node_feat, summed, copies, node_cot, w_node_in, w_node_out
    )
    incoming = assemble(agg_part)
    edge_part, edge_grad, edge_in_grad, edge_out_grad = edge_backward(
        node_feat, edge_feat, offsets, incoming, w_edge_in, w_edge_out, preacts, hiddens
    )
    edge_in_grad, edge_out_grad, node_in_grad, node_out_grad = lax.psum(
        (edge_in_grad, edge_out_grad, node_in_grad, node_out_grad), ("gx", "gy", "gz")
    )
    local = node_cot.astype(jnp.float32) + node_part + edge_part
    node_grad = assemble(local).astype(jnp.bfloat16)
    clipped = clip_all((edge_in_grad, edge_out_grad, node_in_grad, node_out_grad))
    return (node_grad, edge_grad, clipped[0], clipped[1], clipped[2], clipped[3])


def solution(mesh):
    placed = (
        P("gx", "gy", "gz", None),
        P(None, "gx", "gy", "gz", None),
        P("gx", "gy", "gz"),
        P(),
        P(),
        P(),
        P(),
        P(),
        P("gx", "gy", "gz", None),
    )
    return jax.shard_map(
        on_device,
        mesh=mesh,
        in_specs=placed,
        out_specs=(P("gx", "gy", "gz", None), P(None, "gx", "gy", "gz", None), P(), P(), P(), P()),
        check_vma=False,
    )
```

profile of v0, /device:TPU:0, one launch (start us, length us, event | category | flops | bytes accessed | tf_op | source)
XLA Modules:
  0.0 288.3 jit_solution(3967665741030655367)
XLA Ops:
  7.2 0.8 negate_add_fusion
  8.1 0.6 fusion.64
  16.4 0.7 fusion.66
  24.7 0.7 fusion.59
  25.4 1.2 compare_and_fusion.8
  26.6 1.2 compare_and_fusion.10
  28.0 1.4 compare_and_fusion.6
  29.7 1.3 compare_and_fusion.2
  31.0 1.1 compare_and_fusion.4
  32.4 1.3 compare_and_fusion
  41.8 0.4 pad_dynamic-slice_fusion.4
  43.0 0.7 copy-done.4
  45.3 4.9 %collective-permute-start = (f32[1,8,8,128]{3,2,1,0:T(8,128)S(1)}, f32[1,8,8,128]{3,2,1,0:T(8,128)S(1)}, u32[]{:S(2)}, u32[]{:S(2)}) collective-permute-start(f32[1,8,8,128]{3,2,1,0:T(8,128)S(1)} %get-tuple-element.44), channel_id=1, source_target_pairs={{0,16},{1,17},{2,18},{3,19},{4,20},{5,21},{6,22},{7,23},{8,24},{9,... | collective-permute-start | bytes 98312 | tf_op jit(solution)/shard_map/ppermute | solution.py:14
  50.2 1.3 collective-permute-start.1
  51.7 4.2 %collective-permute-done.1 = f32[1,8,8,128]{3,2,1,0:T(8,128)S(1)} collective-permute-done((f32[1,8,8,128]{3,2,1,0:T(8,128)S(1)}, f32[1,8,8,128]{3,2,1,0:T(8,128)S(1)}, u32[]{:S(2)}, u32[]{:S(2)}) %collective-permute-start.1) | collective-permute-done | bytes 32800 | tf_op jit(solution)/shard_map/ppermute | solution.py:17
  56.0 1.3 collective-permute-start.2
  57.3 1.3 collective-permute-start.3
  58.6 0.7 fusion.60
  59.2 2.9 %collective-permute-done.3 = f32[10,1,8,128]{3,2,1,0:T(8,128)S(1)} collective-permute-done((f32[10,1,8,128]{3,2,1,0:T(8,128)S(1)}, f32[10,1,8,128]{3,2,1,0:T(8,128)S(1)}, u32[]{:S(2)}, u32[]{:S(2)}) %collective-permute-start.3) | collective-permute-done | bytes 40992 | tf_op jit(solution)/shard_map/ppermute | solution.py:17
  62.2 3.5 %collective-permute-start.4 = (f32[10,10,1,128]{3,2,1,0:T(1,128)S(1)}, f32[10,10,1,128]{3,2,1,0:T(1,128)S(1)}, u32[]{:S(2)}, u32[]{:S(2)}) collective-permute-start(f32[10,10,1,128]{3,2,1,0:T(1,128)S(1)} %get-tuple-element.28), channel_id=1, source_target_pairs={{0,1},{1,2},{2,3},{4,5},{5,6},{6,7},{8,9},{9,10},{10,11},{12,13},{... | collective-permute-start | bytes 153608 | tf_op jit(solution)/shard_map/ppermute | solution.py:14
  65.7 1.3 collective-permute-start.5
  67.0 0.6 fusion.62
  91.7 0.7 copy-done.9
  92.4 0.9 fusion.20
  93.9 1.6 collective-permute-start.6
  95.5 1.3 collective-permute-start.7
  97.1 4.2 %collective-permute-done.7 = f32[1,8,8,128]{3,2,1,0:T(8,128)S(1)} collective-permute-done((f32[1,8,8,128]{3,2,1,0:T(8,128)S(1)}, f32[1,8,8,128]{3,2,1,0:T(8,128)S(1)}, u32[]{:S(2)}, u32[]{:S(2)}) %collective-permute-start.7) | collective-permute-done | bytes 32800 | tf_op jit(solution)/shard_map/ppermute | solution.py:17
  101.3 2.9 %collective-permute-start.8 = (f32[10,1,8,128]{3,2,1,0:T(8,128)S(1)}, f32[10,1,8,128]{3,2,1,0:T(8,128)S(1)}, u32[]{:S(2)}, u32[]{:S(2)}) collective-permute-start(f32[10,1,8,128]{3,2,1,0:T(8,128)S(1)} %get-tuple-element.32), channel_id=1, source_target_pairs={{0,4},{4,8},{8,12},{1,5},{5,9},{9,13},{2,6},{6,10},{10,14},{3,7},{... | collective-permute-start | bytes 122888 | tf_op jit(solution)/shard_map/ppermute | solution.py:14
  104.2 1.3 collective-permute-start.9
  105.8 2.8 collective-permute-done.9
  108.6 4.6 %collective-permute-start.10 = (f32[10,10,1,128]{3,2,1,0:T(1,128)S(1)}, f32[10,10,1,128]{3,2,1,0:T(1,128)S(1)}, u32[]{:S(2)}, u32[]{:S(2)}) collective-permute-start(f32[10,10,1,128]{3,2,1,0:T(1,128)S(1)} %get-tuple-element.26), channel_id=1, source_target_pairs={{0,1},{1,2},{2,3},{4,5},{5,6},{6,7},{8,9},{9,10},{10,11},{12,13},{... | collective-permute-start | bytes 153608 | tf_op jit(solution)/shard_map/ppermute | solution.py:14
  113.2 1.3 collective-permute-start.11
  114.5 0.7 pad_maximum_fusion.13
  115.2 4.0 %collective-permute-done.11 = f32[10,10,1,128]{3,2,1,0:T(1,128)S(1)} collective-permute-done((f32[10,10,1,128]{3,2,1,0:T(1,128)S(1)}, f32[10,10,1,128]{3,2,1,0:T(1,128)S(1)}, u32[]{:S(2)}, u32[]{:S(2)}) %collective-permute-start.11) | collective-permute-done | bytes 51232 | tf_op jit(solution)/shard_map/ppermute | solution.py:17
  119.9 0.3 fusion.16
  121.3 0.2 convolution_bitcast_fusion.5
  122.6 0.2 convolution_bitcast_fusion.1
  123.1 0.2 convolution_bitcast_fusion.2
  123.6 0.2 convolution_bitcast_fusion.6
  125.6 0.3 convolution_add_fusion.14
  125.9 0.3 convolution_add_fusion.13
  126.1 0.9 convolution_add_fusion.12
  127.6 0.4 fusion.12
  128.0 1.6 collective-permute-start.12
  129.6 1.3 collective-permute-start.13
  131.2 4.6 %collective-permute-done.13 = f32[1,8,8,128]{3,2,1,0:T(8,128)S(1)} collective-permute-done((f32[1,8,8,128]{3,2,1,0:T(8,128)S(1)}, f32[1,8,8,128]{3,2,1,0:T(8,128)S(1)}, u32[]{:S(2)}, u32[]{:S(2)}) %collective-permute-start.13) | collective-permute-done | bytes 32800 | tf_op jit(solution)/shard_map/ppermute | solution.py:17
  135.8 2.0 collective-permute-start.14
  137.8 1.3 collective-permute-start.15
  139.1 0.7 fusion.19
  139.8 2.8 collective-permute-done.15
  142.7 3.5 %collective-permute-start.16 = (f32[10,10,1,128]{3,2,1,0:T(1,128)S(1)}, f32[10,10,1,128]{3,2,1,0:T(1,128)S(1)}, u32[]{:S(2)}, u32[]{:S(2)}) collective-permute-start(f32[10,10,1,128]{3,2,1,0:T(1,128)S(1)} %get-tuple-element.24), channel_id=1, source_target_pairs={{0,1},{1,2},{2,3},{4,5},{5,6},{6,7},{8,9},{9,10},{10,11},{12,13},{... | collective-permute-start | bytes 153608 | tf_op jit(solution)/shard_map/ppermute | solution.py:14
  146.2 1.3 collective-permute-start.17
  147.5 0.9 pad_maximum_fusion.9
  148.4 3.8 %collective-permute-done.17 = f32[10,10,1,128]{3,2,1,0:T(1,128)S(1)} collective-permute-done((f32[10,10,1,128]{3,2,1,0:T(1,128)S(1)}, f32[10,10,1,128]{3,2,1,0:T(1,128)S(1)}, u32[]{:S(2)}, u32[]{:S(2)}) %collective-permute-start.17) | collective-permute-done | bytes 51232 | tf_op jit(solution)/shard_map/ppermute | solution.py:17
  152.8 0.8 pad_maximum_fusion.12
  153.6 117.3 %all-reduce.8.cloned.1.call-done = (f32[384,128]{1,0:T(8,128)}, f32[128,128]{1,0:T(8,128)}, f32[256,128]{1,0:T(8,128)}, f32[128,128]{1,0:T(8,128)}) async-done(((f32[384,128]{1,0:T(8,128)}, f32[128,128]{1,0:T(8,128)}, f32[256,128]{1,0:T(8,128)}, f32[128,128]{1,0:T(8,128)}), (f32[384,128]{1,0:T(8,128)}, f32[128,128]{1,0:T(8,128)}, f32[256,128]{1,0:T(8,128)}, ...) | async-done | bytes 458768 | tf_op jit(solution)/shard_map/psum | solution.py:194
  270.8 1.5 multiply_reduce_fusion.2
  272.3 1.5 multiply_reduce_fusion.1
  273.9 1.5 multiply_reduce_fusion.3
  275.4 0.6 multiply_reduce_fusion
  278.6 0.6 broadcast_multiply_fusion.2
  279.3 0.7 broadcast_multiply_fusion.1
  280.1 0.6 broadcast_multiply_fusion.3
  280.8 0.7 broadcast_multiply_fusion
  (139 shorter events, 12.4 us)
Async XLA Ops:
  7.2 37.3 %copy-start = (bf16[128,128]{1,0:T(8,128)(2,1)S(1)}, bf16[128,128]{1,0:T(8,128)(2,1)}, u32[]{:S(2)}) copy-start(bf16[128,128]{1,0:T(8,128)(2,1)} %param.14) | copy-start | bytes 98308
  7.2 263.7 %all-reduce.8.cloned.1.call-start = ((), (), s32[]{:S(2)}) async-start(), calls=%async_computation | async-start | bytes 917504 | tf_op jit(solution)/shard_map/psum | solution.py:194
  23.4 1.3 copy-start.10
  29.5 12.1 %copy-start.1 = (bf16[8,8,8,128]{3,2,1,0:T(8,128)(2,1)S(1)}, bf16[8,8,8,128]{3,2,1,0:T(8,128)(2,1)}, u32[]{:S(2)}) copy-start(bf16[8,8,8,128]{3,2,1,0:T(8,128)(2,1)} %param.9) | copy-start | bytes 393220
  31.0 10.7 %copy-start.2 = (bf16[384,128]{1,0:T(8,128)(2,1)S(1)}, bf16[384,128]{1,0:T(8,128)(2,1)}, u32[]{:S(2)}) copy-start(bf16[384,128]{1,0:T(8,128)(2,1)} %param.13) | copy-start | bytes 294916
  42.6 1.0 copy-start.4
  45.2 6.2 %copy-start.8 = (bf16[256,128]{1,0:T(8,128)(2,1)S(1)}, bf16[256,128]{1,0:T(8,128)(2,1)}, u32[]{:S(2)}) copy-start(bf16[256,128]{1,0:T(8,128)(2,1)} %param.15) | copy-start | bytes 196612
  45.3 6.5 %collective-permute-start = (f32[1,8,8,128]{3,2,1,0:T(8,128)S(1)}, f32[1,8,8,128]{3,2,1,0:T(8,128)S(1)}, u32[]{:S(2)}, u32[]{:S(2)}) collective-permute-start(f32[1,8,8,128]{3,2,1,0:T(8,128)S(1)} %get-tuple-element.44), channel_id=1, source_target_pairs={{0,16},{1,17},{2,18},{3,19},{4,20},{5,21},{6,22},{7,23},{8,24},{9,... | collective-permute-start | bytes 98312 | tf_op jit(solution)/shard_map/ppermute | solution.py:14
  50.2 5.8 %collective-permute-start.1 = (f32[1,8,8,128]{3,2,1,0:T(8,128)S(1)}, f32[1,8,8,128]{3,2,1,0:T(8,128)S(1)}, u32[]{:S(2)}, u32[]{:S(2)}) collective-permute-start(f32[1,8,8,128]{3,2,1,0:T(8,128)S(1)} %get-tuple-element.45), channel_id=1, source_target_pairs={{16,0},{17,1},{18,2},{19,3},{20,4},{21,5},{22,6},{23,7},{24,8},{25... | collective-permute-start | bytes 98312 | tf_op jit(solution)/shard_map/ppermute | solution.py:17
  56.0 3.3 %collective-permute-start.2 = (f32[10,1,8,128]{3,2,1,0:T(8,128)S(1)}, f32[10,1,8,128]{3,2,1,0:T(8,128)S(1)}, u32[]{:S(2)}, u32[]{:S(2)}) collective-permute-start(f32[10,1,8,128]{3,2,1,0:T(8,128)S(1)} %get-tuple-element.34), channel_id=1, source_target_pairs={{0,4},{4,8},{8,12},{1,5},{5,9},{9,13},{2,6},{6,10},{10,14},{3,7},{... | collective-permute-start | bytes 122888 | tf_op jit(solution)/shard_map/ppermute | solution.py:14
  57.3 4.9 %collective-permute-start.3 = (f32[10,1,8,128]{3,2,1,0:T(8,128)S(1)}, f32[10,1,8,128]{3,2,1,0:T(8,128)S(1)}, u32[]{:S(2)}, u32[]{:S(2)}) collective-permute-start(f32[10,1,8,128]{3,2,1,0:T(8,128)S(1)} %get-tuple-element.35), channel_id=1, source_target_pairs={{4,0},{8,4},{12,8},{5,1},{9,5},{13,9},{6,2},{10,6},{14,10},{7,3},{... | collective-permute-start | bytes 122888 | tf_op jit(solution)/shard_map/ppermute | solution.py:17
  62.2 28.5 %collective-permute-start.4 = (f32[10,10,1,128]{3,2,1,0:T(1,128)S(1)}, f32[10,10,1,128]{3,2,1,0:T(1,128)S(1)}, u32[]{:S(2)}, u32[]{:S(2)}) collective-permute-start(f32[10,10,1,128]{3,2,1,0:T(1,128)S(1)} %get-tuple-element.28), channel_id=1, source_target_pairs={{0,1},{1,2},{2,3},{4,5},{5,6},{6,7},{8,9},{9,10},{10,11},{12,13},{... | collective-permute-start | bytes 153608 | tf_op jit(solution)/shard_map/ppermute | solution.py:14
  65.7 25.0 %collective-permute-start.5 = (f32[10,10,1,128]{3,2,1,0:T(1,128)S(1)}, f32[10,10,1,128]{3,2,1,0:T(1,128)S(1)}, u32[]{:S(2)}, u32[]{:S(2)}) collective-permute-start(f32[10,10,1,128]{3,2,1,0:T(1,128)S(1)} %get-tuple-element.29), channel_id=1, source_target_pairs={{1,0},{2,1},{3,2},{5,4},{6,5},{7,6},{9,8},{10,9},{11,10},{13,12},{... | collective-permute-start | bytes 153608 | tf_op jit(solution)/shard_map/ppermute | solution.py:17
  71.5 11.4 %copy-start.11 = (s32[8,8,8]{2,1,0:T(8,128)S(1)}, s32[8,8,8]{2,1,0:T(8,128)}, u32[]{:S(2)}) copy-start(s32[8,8,8]{2,1,0:T(8,128)} %param.11) | copy-start | bytes 6148
  91.5 0.9 copy-start.9
  92.4 0.9 copy-start.12
  93.9 3.2 %collective-permute-start.6 = (f32[1,8,8,128]{3,2,1,0:T(8,128)S(1)}, f32[1,8,8,128]{3,2,1,0:T(8,128)S(1)}, u32[]{:S(2)}, u32[]{:S(2)}) collective-permute-start(f32[1,8,8,128]{3,2,1,0:T(8,128)S(1)} %get-tuple-element.42), channel_id=1, source_target_pairs={{0,16},{1,17},{2,18},{3,19},{4,20},{5,21},{6,22},{7,23},{8,24},{9,... | collective-permute-start | bytes 98312 | tf_op jit(solution)/shard_map/ppermute | solution.py:14
  95.5 5.8 %collective-permute-start.7 = (f32[1,8,8,128]{3,2,1,0:T(8,128)S(1)}, f32[1,8,8,128]{3,2,1,0:T(8,128)S(1)}, u32[]{:S(2)}, u32[]{:S(2)}) collective-permute-start(f32[1,8,8,128]{3,2,1,0:T(8,128)S(1)} %get-tuple-element.43), channel_id=1, source_target_pairs={{16,0},{17,1},{18,2},{19,3},{20,4},{21,5},{22,6},{23,7},{24,8},{25... | collective-permute-start | bytes 98312 | tf_op jit(solution)/shard_map/ppermute | solution.py:17
  101.3 4.4 %collective-permute-start.8 = (f32[10,1,8,128]{3,2,1,0:T(8,128)S(1)}, f32[10,1,8,128]{3,2,1,0:T(8,128)S(1)}, u32[]{:S(2)}, u32[]{:S(2)}) collective-permute-start(f32[10,1,8,128]{3,2,1,0:T(8,128)S(1)} %get-tuple-element.32), channel_id=1, source_target_pairs={{0,4},{4,8},{8,12},{1,5},{5,9},{9,13},{2,6},{6,10},{10,14},{3,7},{... | collective-permute-start | bytes 122888 | tf_op jit(solution)/shard_map/ppermute | solution.py:14
  104.2 4.3 %collective-permute-start.9 = (f32[10,1,8,128]{3,2,1,0:T(8,128)S(1)}, f32[10,1,8,128]{3,2,1,0:T(8,128)S(1)}, u32[]{:S(2)}, u32[]{:S(2)}) collective-permute-start(f32[10,1,8,128]{3,2,1,0:T(8,128)S(1)} %get-tuple-element.33), channel_id=1, source_target_pairs={{4,0},{8,4},{12,8},{5,1},{9,5},{13,9},{6,2},{10,6},{14,10},{7,3},{... | collective-permute-start | bytes 122888 | tf_op jit(solution)/shard_map/ppermute | solution.py:17
  108.6 6.5 %collective-permute-start.10 = (f32[10,10,1,128]{3,2,1,0:T(1,128)S(1)}, f32[10,10,1,128]{3,2,1,0:T(1,128)S(1)}, u32[]{:S(2)}, u32[]{:S(2)}) collective-permute-start(f32[10,10,1,128]{3,2,1,0:T(1,128)S(1)} %get-tuple-element.26), channel_id=1, source_target_pairs={{0,1},{1,2},{2,3},{4,5},{5,6},{6,7},{8,9},{9,10},{10,11},{12,13},{... | collective-permute-start | bytes 153608 | tf_op jit(solution)/shard_map/ppermute | solution.py:14
  113.2 6.0 %collective-permute-start.11 = (f32[10,10,1,128]{3,2,1,0:T(1,128)S(1)}, f32[10,10,1,128]{3,2,1,0:T(1,128)S(1)}, u32[]{:S(2)}, u32[]{:S(2)}) collective-permute-start(f32[10,10,1,128]{3,2,1,0:T(1,128)S(1)} %get-tuple-element.27), channel_id=1, source_target_pairs={{1,0},{2,1},{3,2},{5,4},{6,5},{7,6},{9,8},{10,9},{11,10},{13,12},{... | collective-permute-start | bytes 153608 | tf_op jit(solution)/shard_map/ppermute | solution.py:17
  128.0 3.2 %collective-permute-start.12 = (f32[1,8,8,128]{3,2,1,0:T(8,128)S(1)}, f32[1,8,8,128]{3,2,1,0:T(8,128)S(1)}, u32[]{:S(2)}, u32[]{:S(2)}) collective-permute-start(f32[1,8,8,128]{3,2,1,0:T(8,128)S(1)} %get-tuple-element.36), channel_id=1, source_target_pairs={{0,16},{1,17},{2,18},{3,19},{4,20},{5,21},{6,22},{7,23},{8,24},{9,... | collective-permute-start | bytes 98312 | tf_op jit(solution)/shard_map/ppermute | solution.py:14
  129.6 6.1 %collective-permute-start.13 = (f32[1,8,8,128]{3,2,1,0:T(8,128)S(1)}, f32[1,8,8,128]{3,2,1,0:T(8,128)S(1)}, u32[]{:S(2)}, u32[]{:S(2)}) collective-permute-start(f32[1,8,8,128]{3,2,1,0:T(8,128)S(1)} %get-tuple-element.37), channel_id=1, source_target_pairs={{16,0},{17,1},{18,2},{19,3},{20,4},{21,5},{22,6},{23,7},{24,8},{25... | collective-permute-start | bytes 98312 | tf_op jit(solution)/shard_map/ppermute | solution.py:17
  135.8 4.1 %collective-permute-start.14 = (f32[10,1,8,128]{3,2,1,0:T(8,128)S(1)}, f32[10,1,8,128]{3,2,1,0:T(8,128)S(1)}, u32[]{:S(2)}, u32[]{:S(2)}) collective-permute-start(f32[10,1,8,128]{3,2,1,0:T(8,128)S(1)} %get-tuple-element.30), channel_id=1, source_target_pairs={{0,4},{4,8},{8,12},{1,5},{5,9},{9,13},{2,6},{6,10},{10,14},{3,7},{... | collective-permute-start | bytes 122888 | tf_op jit(solution)/shard_map/ppermute | solution.py:14
  137.8 4.9 %collective-permute-start.15 = (f32[10,1,8,128]{3,2,1,0:T(8,128)S(1)}, f32[10,1,8,128]{3,2,1,0:T(8,128)S(1)}, u32[]{:S(2)}, u32[]{:S(2)}) collective-permute-start(f32[10,1,8,128]{3,2,1,0:T(8,128)S(1)} %get-tuple-element.31), channel_id=1, source_target_pairs={{4,0},{8,4},{12,8},{5,1},{9,5},{13,9},{6,2},{10,6},{14,10},{7,3},{... | collective-permute-start | bytes 122888 | tf_op jit(solution)/shard_map/ppermute | solution.py:17
  142.7 5.7 %collective-permute-start.16 = (f32[10,10,1,128]{3,2,1,0:T(1,128)S(1)}, f32[10,10,1,128]{3,2,1,0:T(1,128)S(1)}, u32[]{:S(2)}, u32[]{:S(2)}) collective-permute-start(f32[10,10,1,128]{3,2,1,0:T(1,128)S(1)} %get-tuple-element.24), channel_id=1, source_target_pairs={{0,1},{1,2},{2,3},{4,5},{5,6},{6,7},{8,9},{9,10},{10,11},{12,13},{... | collective-permute-start | bytes 153608 | tf_op jit(solution)/shard_map/ppermute | solution.py:14
  146.2 6.0 %collective-permute-start.17 = (f32[10,10,1,128]{3,2,1,0:T(1,128)S(1)}, f32[10,10,1,128]{3,2,1,0:T(1,128)S(1)}, u32[]{:S(2)}, u32[]{:S(2)}) collective-permute-start(f32[10,10,1,128]{3,2,1,0:T(1,128)S(1)} %get-tuple-element.25), channel_id=1, source_target_pairs={{1,0},{2,1},{3,2},{5,4},{6,5},{7,6},{9,8},{10,9},{11,10},{13,12},{... | collective-permute-start | bytes 153608 | tf_op jit(solution)/shard_map/ppermute | solution.py:17
  270.8 4.5 %copy-start.3 = (f32[384,128]{1,0:T(8,128)S(1)}, f32[384,128]{1,0:T(8,128)}, u32[]{:S(2)}) copy-start(f32[384,128]{1,0:T(8,128)} %get-tuple-element.6) | copy-start | bytes 589828
  275.3 3.3 %copy-start.7 = (f32[128,128]{1,0:T(8,128)S(1)}, f32[128,128]{1,0:T(8,128)}, u32[]{:S(2)}) copy-start(f32[128,128]{1,0:T(8,128)} %get-tuple-element.9) | copy-start | bytes 196612
  275.4 3.9 %copy-start.5 = (f32[256,128]{1,0:T(8,128)S(1)}, f32[256,128]{1,0:T(8,128)}, u32[]{:S(2)}) copy-start(f32[256,128]{1,0:T(8,128)} %get-tuple-element.8) | copy-start | bytes 393220
  279.3 0.8 copy-start.6
Sparse Core Ops, SparseCore 0:
  139.9 130.8 all-reduce.7
where the time goes:
time: 290 us; the launch traced here: 288 us
  waiting for transfers between devices  147 us (51%)
  between operations  63.6 us (22%)
  starting transfers between devices  37.5 us (13%)
  other arithmetic  22.3 us (8%)
  matrix products  12 us (4%)
  local copies, waits for them, and re-layouts  6.04 us (2%)
    psum x1, waiting for transfers between devices, on_device(): lax.psum((edge_in_grad, edge_out_grad, node_in_grad, node_out_grad), ('gx...  117 us
    ppermute x9, waiting for transfers between devices, extended(): lax.ppermute(lax.slice_in_dim(block, 0, width, axis=dim), axis, backward)  29.4 us
    ppermute x9, starting transfers between devices, extended(): lax.ppermute(lax.slice_in_dim(block, block.shape[dim] - width, None, axis...  25.8 us
    ppermute x9, starting transfers between devices, extended(): lax.ppermute(lax.slice_in_dim(block, 0, width, axis=dim), axis, backward)  11.6 us
    and x6, other arithmetic, neighbour_valid(): (coords + offset[which] >= 0) & (coords + offset[which] < brick)  7.56 us
  transfers between devices with their start and end apart: 19, of which 11 were waited for; matrix products, arithmetic and copies ran while one was open for 2% of the time, Pallas kernels for 0%

commit v1 on v0

v1 whole, which is shorter than its diff:
```python
import functools
import math

import jax
import jax.numpy as jnp
from jax import lax
from jax.experimental import pallas as pl
from jax.experimental.pallas import tpu as pltpu
from jax.sharding import PartitionSpec as P

F32 = jnp.float32
BF16 = jnp.bfloat16
AXES = ("gx", "gy", "gz")
DIRS = [
    (dx, dy, dz)
    for dx in (-1, 0, 1)
    for dy in (-1, 0, 1)
    for dz in (-1, 0, 1)
    if (dx, dy, dz) != (0, 0, 0)
]


def dot(left, right):
    return jnp.dot(left, right, preferred_element_type=F32)


def dot_t(left, right):
    return lax.dot_general(left, right, (((1,), (1,)), ((), ())), preferred_element_type=F32)


def outer(left, right):
    return lax.dot_general(left, right, (((0,), (0,)), ((), ())), preferred_element_type=F32)


def class_slot(d):
    slot = 0
    for step in d:
        if step != 0:
            slot = slot * 2 + (0 if step < 0 else 1)
    return "".join("xyz"[i] for i in range(3) if d[i] != 0), slot


def part(ref, lead, d, edge, low):
    where = list(lead)
    for step in d[:2]:
        if step == 0:
            where.append(slice(None))
        else:
            where.append(edge if (step > 0) != low else 0)
    return ref.at[tuple(where)]


def kernel(
    sizes, group, rest,
    offs, node_ref, edge_ref, cop_ref, wei, weo, wni, wno, cot_ref,
    o_node, o_edge, o_ei, o_eo, o_ni, o_no,
    edges, egr, pad_a, pad_s, sl, hs, field, zs, field2,
    rx, ry, rz, rxy, rxz, ryz, rxyz,
    ng, eg, gn, ge, rbn, rbe, exn, exe,
    in_sem, out_sem, hs_sem, hr_sem, rs_s, rs_r, ex_s, ex_r, ag_s, ag_r,
):
    width = node_ref.shape[1]
    count = node_ref.shape[0]
    brick = field.shape[1]
    kinds = offs.shape[0]
    edge = brick - 1
    cube = (brick, brick, brick, width)
    pos = {a: lax.axis_index(a) for a in AXES}
    recv = {"x": rx, "y": ry, "z": rz, "xy": rxy, "xz": rxz, "yz": ryz, "xyz": rxyz}

    fetch = pltpu.make_async_copy(edge_ref, edges, in_sem)
    fetch.start()

    def exists(d, sign):
        ok = None
        for a, step in zip(AXES, d):
            if step != 0:
                here = pos[a] + sign * step
                one = (here >= 0) & (here < sizes[a])
                ok = one if ok is None else ok & one
        return ok

    def shifted(d, sign):
        return {a: pos[a] + sign * step for a, step in zip(AXES, d)}

    def rank_of(axes):
        rank = 0
        for a in axes:
            rank = rank * sizes[a] + pos[a]
        return rank

    def place_of(axes, rank):
        place = dict(pos)
        for a in reversed(axes):
            place[a] = lax.rem(rank, sizes[a])
            rank = rank // sizes[a]
        return place

    members = math.prod(sizes[a] for a in group)
    me = rank_of(group)

    barrier = pltpu.get_barrier_semaphore()

    def greet(place):
        pl.semaphore_signal(
            barrier, inc=1, device_id=place, device_id_type=pl.DeviceIdType.MESH
        )

    waits = jnp.int32(members - 1 + sum(sizes[a] - 1 for a in rest))
    for j in range(1, members):
        greet(place_of(group, lax.rem(me + j, members)))
    for a in rest:
        for j in range(1, sizes[a]):
            greet(place_of((a,), lax.rem(pos[a] + j, sizes[a])))
    for d in DIRS:
        ok = exists(d, 1)
        waits = waits + ok.astype(jnp.int32)

        @pl.when(ok)
        def _(d=d):
            greet(shifted(d, 1))

    def halo_copy(a, i, d, place):
        name, slot = class_slot(d)
        if d[2] == 0:
            src = part(field, (a,), d, edge, False)
        else:
            src = part(zs, (a, 0 if d[2] < 0 else 1), d, edge, False)
        return pltpu.make_async_remote_copy(
            src_ref=src,
            dst_ref=recv[name].at[a, slot],
            send_sem=hs_sem.at[a, i],
            recv_sem=hr_sem.at[a, i],
            device_id=place,
            device_id_type=pl.DeviceIdType.MESH,
        )

    def halo_start(a, values):
        values = values.reshape(cube)
        field[a] = values
        zs[a, 0] = values[:, :, 0:1, :]
        zs[a, 1] = values[:, :, edge:, :]
        for i, d in enumerate(DIRS):

            @pl.when(exists(d, 1))
            def _(i=i, d=d):
                halo_copy(a, i, d, shifted(d, 1)).start()

        field2[a] = values

    def halo_finish(a):
        for i, d in enumerate(DIRS):

            @pl.when(exists(d, -1))
            def _(i=i, d=d):
                halo_copy(a, i, d, shifted(d, -1)).wait_recv()
                name, slot = class_slot(d)
                where = [a]
                for step in d[:2]:
                    where.append(slice(None) if step == 0 else (0 if step > 0 else edge))
                if d[2] != 0:
                    where.append(slice(0, 1) if d[2] > 0 else slice(edge, brick))
                where = tuple(where)
                field2[where] = field2[where] + recv[name][a, slot]

        return field2[a].reshape(count, width)

    def halo_drain(a):
        for i, d in enumerate(DIRS):

            @pl.when(exists(d, 1))
            def _(i=i, d=d):
                halo_copy(a, i, d, shifted(d, 1)).wait_send()

    def rows_at(ref, rank, rows):
        return ref.at[pl.ds(pl.multiple_of(rank * rows, 8), rows)]

    def rs_copy(w, j):
        src, dst = (ng, rbn) if w == 0 else (eg, rbe)
        to = lax.rem(me + j, members)
        rows = src.shape[0] // members
        return pltpu.make_async_remote_copy(
            src_ref=rows_at(src, to, rows),
            dst_ref=dst.at[j],
            send_sem=rs_s.at[w, j],
            recv_sem=rs_r.at[w, j],
            device_id=place_of(group, to),
            device_id_type=pl.DeviceIdType.MESH,
        )

    def rs_start(w):
        for j in range(1, members):
            rs_copy(w, j).start()

    def rs_finish(w):
        src, dst = (ng, rbn) if w == 0 else (eg, rbe)
        rows = src.shape[0] // members
        total = rows_at(src, me, rows)[...]
        for j in range(1, members):
            rs_copy(w, j).wait_recv()
            total = total + dst[j]
        return total

    bases = []
    base = 0
    for a in rest:
        bases.append(base)
        base += sizes[a]

    def ex_copy(w, e, j):
        buf = exn if w == 0 else exe
        a = rest[e]
        spot = buf.at[bases[e] + pos[a]]
        return pltpu.make_async_remote_copy(
            src_ref=spot,
            dst_ref=spot,
            send_sem=ex_s.at[w, bases[e] + j],
            recv_sem=ex_r.at[w, bases[e] + j],
            device_id=place_of((a,), lax.rem(pos[a] + j, sizes[a])),
            device_id_type=pl.DeviceIdType.MESH,
        )

    def ex_start(w, e, total):
        buf = exn if w == 0 else exe
        buf[bases[e] + pos[rest[e]]] = total
        for j in range(1, sizes[rest[e]]):
            ex_copy(w, e, j).start()

    def ex_finish(w, e):
        buf = exn if w == 0 else exe
        for j in range(1, sizes[rest[e]]):
            ex_copy(w, e, j).wait_recv()
        total = buf[bases[e]]
        for r in range(1, sizes[rest[e]]):
            total = total + buf[bases[e] + r]
        return total

    def ex_all(w):
        for e in range(len(rest)):
            total = ex_finish(w, e)
            if e + 1 < len(rest):
                ex_start(w, e + 1, total)
        return total

    def ag_copy(w, j):
        buf = gn if w == 0 else ge
        spot = rows_at(buf, me, buf.shape[0] // members)
        return pltpu.make_async_remote_copy(
            src_ref=spot,
            dst_ref=spot,
            send_sem=ag_s.at[w, j],
            recv_sem=ag_r.at[w, j],
            device_id=place_of(group, lax.rem(me + j, members)),
            device_id_type=pl.DeviceIdType.MESH,
        )

    def ag_start(w, total):
        buf = gn if w == 0 else ge
        rows_at(buf, me, buf.shape[0] // members)[...] = total
        for j in range(1, members):
            ag_copy(w, j).start()

    def ag_finish(w):
        for j in range(1, members):
            ag_copy(w, j).wait_recv()

    node = node_ref[...]
    pad_a[...] = jnp.zeros_like(pad_a)
    pad_s[...] = jnp.zeros_like(pad_s)
    pad_a[1 : brick + 1, 1 : brick + 1] = dot(node, wei[:width]).reshape(cube)
    received = dot(node, wei[width : 2 * width])
    coords = [lax.broadcasted_iota(jnp.int32, cube, axis) for axis in range(3)]
    scale_rows = lax.broadcasted_iota(jnp.int32, (count, brick * brick), 0) // brick
    scale_cols = lax.broadcasted_iota(jnp.int32, (count, brick * brick), 1)
    picked = dot(
        (scale_rows == scale_cols).astype(BF16), cop_ref[...].astype(F32).astype(BF16)
    )
    lane = lax.broadcasted_iota(jnp.int32, (count, brick), 1)
    row = lax.broadcasted_iota(jnp.int32, (count, brick), 0) % brick
    picked = jnp.where(lane == row, picked, 0.0).astype(BF16)
    inverse = 1.0 / dot(picked, jnp.ones((brick, width), BF16))
    fetch.wait()
    hiddens = []
    hidden_sum = None
    for k in range(kinds):
        o = [offs[k, axis] for axis in range(3)]
        sent = pad_a[pl.ds(1 + o[0], brick), pl.ds(1 + o[1], brick)]
        sent = pltpu.roll(sent.reshape(brick * brick, brick, width), lax.rem(brick - o[2], brick), 1)
        pre = dot(edges[k * count : (k + 1) * count], wei[2 * width :])
        pre = pre + received + sent.reshape(count, width)
        sigma = 0.5 * jnp.tanh(0.5 * pre) + 0.5
        hidden = pre * sigma
        valid = None
        for axis in range(3):
            here = coords[axis] + o[axis]
            one = (here >= 0) & (here < brick)
            valid = one if valid is None else valid & one
        valid = valid.reshape(count, width)
        sl[k] = jnp.where(valid, sigma + hidden * (1.0 - sigma), 0.0)
        hidden = jnp.where(valid, hidden, 0.0).astype(BF16)
        hiddens.append(hidden)
        wide = hidden.astype(F32)
        hidden_sum = wide if hidden_sum is None else hidden_sum + wide
    w_out = weo[...]
    local_sum = dot(
        jnp.concatenate(hiddens, axis=1), jnp.concatenate([w_out] * kinds, axis=0)
    )
    pl.semaphore_wait(barrier, waits)
    halo_start(0, local_sum)

    hs[...] = hidden_sum.astype(BF16)
    cot = cot_ref[...]
    node_own = dot(node, wni[:width])
    upstream = dot_t(cot, wno[...])

    summed = halo_finish(0)
    gathered = (summed * inverse).astype(BF16)
    pre = node_own + dot(gathered, wni[width:])
    sigma = 0.5 * jnp.tanh(0.5 * pre) + 0.5
    hidden = pre * sigma
    slope = (upstream * (sigma + hidden * (1.0 - sigma))).astype(BF16)
    halo_start(1, dot_t(slope, wni[width:]) * inverse)
    ng[:width] = outer(node, slope)
    ng[width : 2 * width] = outer(gathered, slope)
    ng[2 * width :] = outer(hidden.astype(BF16), cot)
    rs_start(0)
    own = cot.astype(F32) + dot_t(slope, wni[:width])

    arriving = halo_finish(1).astype(BF16)
    back = dot_t(arriving, w_out)
    slopes = []
    direct = None
    turned = None
    for k in range(kinds):
        o = [offs[k, axis] for axis in range(3)]
        slope = (back * sl[k]).astype(BF16)
        slopes.append(slope)
        wide = slope.astype(F32)
        direct = wide if direct is None else direct + wide
        pad_s[k, 1 : brick + 1, 1 : brick + 1] = wide.reshape(cube)
        moved = pad_s[k, pl.ds(1 - o[0], brick), pl.ds(1 - o[1], brick)]
        moved = pltpu.roll(moved.reshape(brick * brick, brick, width), lax.rem(brick + o[2], brick), 1)
        turned = moved if turned is None else turned + moved
    turned = turned.reshape(count, width).astype(BF16)
    direct = direct.astype(BF16)
    slope_all = jnp.concatenate(slopes, axis=0)
    eg[:width] = outer(node, turned)
    eg[width : 2 * width] = outer(node, direct)
    eg[2 * width : 3 * width] = outer(edges[...], slope_all)
    eg[3 * width :] = outer(hs[...], arriving)
    rs_start(1)
    own = own + dot_t(turned, wei[:width]) + dot_t(direct, wei[width : 2 * width])
    halo_start(2, own)
    ex_start(0, 0, rs_finish(0))
    egr[...] = dot_t(slope_all, wei[2 * width :]).astype(BF16)
    store = pltpu.make_async_copy(egr, o_edge, out_sem)
    store.start()
    ex_start(1, 0, rs_finish(1))
    ag_start(0, ex_all(0))
    o_node[...] = halo_finish(2).astype(BF16)
    ag_start(1, ex_all(1))
    ag_finish(0)
    node_total = gn[...]
    squares = jnp.sum(node_total * node_total, axis=0, keepdims=True)
    ag_finish(1)
    edge_total = ge[...]
    squares = squares + jnp.sum(edge_total * edge_total, axis=0, keepdims=True)
    squares = jnp.sum(squares, axis=1, keepdims=True)
    entries = (ge.shape[0] + gn.shape[0]) * width
    factor = math.sqrt(entries) / jnp.sqrt(squares)
    o_ei[...] = edge_total[: 3 * width] * factor
    o_eo[...] = edge_total[3 * width :] * factor
    o_ni[...] = node_total[: 2 * width] * factor
    o_no[...] = node_total[2 * width :] * factor
    store.wait()
    for a in range(3):
        halo_drain(a)
    for w in range(2):
        for j in range(1, members):
            rs_copy(w, j).wait_send()
            ag_copy(w, j).wait_send()
        for e in range(len(rest)):
            for j in range(1, sizes[rest[e]]):
                ex_copy(w, e, j).wait_send()


def on_device(
    sizes, node_feat, edge_feat, copies, offsets, w_edge_in, w_edge_out, w_node_in, w_node_out, node_cot
):
    brick = node_feat.shape[0]
    width = node_feat.shape[3]
    kinds = edge_feat.shape[0]
    count = brick**3
    rows_n, rows_e = 3 * width, 4 * width
    group, rest = ("gx", "gy"), ("gz",)
    if math.gcd(rows_n, rows_e) % (8 * sizes["gx"] * sizes["gy"]) != 0:
        group, rest = ("gy",), ("gx", "gz")
    members = math.prod(sizes[a] for a in group)
    others = sum(sizes[a] for a in rest)
    vmem = pl.BlockSpec(memory_space=pltpu.VMEM)
    smem = pl.BlockSpec(memory_space=pltpu.SMEM)
    hbm = pl.BlockSpec(memory_space=pl.ANY)
    dma = pltpu.SemaphoreType.DMA
    b, w = brick, width
    outs = pl.pallas_call(
        functools.partial(kernel, sizes, group, rest),
        out_shape=(
            jax.ShapeDtypeStruct((count, w), BF16),
            jax.ShapeDtypeStruct((kinds * count, w), BF16),
            jax.ShapeDtypeStruct((3 * w, w), F32),
            jax.ShapeDtypeStruct((w, w), F32),
            jax.ShapeDtypeStruct((2 * w, w), F32),
            jax.ShapeDtypeStruct((w, w), F32),
        ),
        in_specs=[smem, vmem, hbm, vmem, vmem, vmem, vmem, vmem, vmem],
        out_specs=(vmem, hbm, vmem, vmem, vmem, vmem),
        scratch_shapes=[
            pltpu.VMEM((kinds * count, w), BF16),
            pltpu.VMEM((kinds * count, w), BF16),
            pltpu.VMEM((b + 2, b + 2, b, w), F32),
            pltpu.VMEM((kinds, b + 2, b + 2, b, w), F32),
            pltpu.VMEM((kinds, count, w), F32),
            pltpu.VMEM((count, w), BF16),
            pltpu.VMEM((3, b, b, b, w), F32),
            pltpu.VMEM((3, 2, b, b, 1, w), F32),
            pltpu.VMEM((3, b, b, b, w), F32),
            pltpu.VMEM((3, 2, b, b, w), F32),
            pltpu.VMEM((3, 2, b, b, w), F32),
            pltpu.VMEM((3, 2, b, b, 1, w), F32),
            pltpu.VMEM((3, 4, b, w), F32),
            pltpu.VMEM((3, 4, b, 1, w), F32),
            pltpu.VMEM((3, 4, b, 1, w), F32),
            pltpu.VMEM((3, 8, 1, w), F32),
            pltpu.VMEM((rows_n, w), F32),
            pltpu.VMEM((rows_e, w), F32),
            pltpu.VMEM((rows_n, w), F32),
            pltpu.VMEM((rows_e, w), F32),
            pltpu.VMEM((members, rows_n // members, w), F32),
            pltpu.VMEM((members, rows_e // members, w), F32),
            pltpu.VMEM((others, rows_n // members, w), F32),
            pltpu.VMEM((others, rows_e // members, w), F32),
            dma,
            dma,
            dma((3, len(DIRS))),
            dma((3, len(DIRS))),
            dma((2, members)),
            dma((2, members)),
            dma((2, others)),
            dma((2, others)),
            dma((2, members)),
            dma((2, members)),
        ],
        compiler_params=pltpu.CompilerParams(collective_id=0, has_side_effects=True),
    )(
        offsets,
        node_feat.reshape(count, w),
        edge_feat.reshape(kinds * count, w),
        copies.reshape(b * b, b),
        w_edge_in,
        w_edge_out,
        w_node_in,
        w_node_out,
        node_cot.reshape(count, w),
    )
    return (outs[0].reshape(node_feat.shape), outs[1].reshape(edge_feat.shape)) + tuple(outs[2:])


def solution(mesh):
    sizes = {a: mesh.shape[a] for a in AXES}
    bricks, edges = P("gx", "gy", "gz", None), P(None, "gx", "gy", "gz", None)
    return jax.shard_map(
        functools.partial(on_device, sizes),
        mesh=mesh,
        in_specs=(bricks, edges, P("gx", "gy", "gz"), P(), P(), P(), P(), P(), bricks),
        out_specs=(bricks, edges, P(), P(), P(), P()),
        check_vma=False,
    )
```

time: 290 us -> 40.4 us (0.14)
  waiting for transfers between devices: 147 us -> 0 us
  between operations: 63.6 us -> 0.65 us
  starting transfers between devices: 37.5 us -> 0 us
  Pallas kernels: 0 us -> 32.7 us
  other arithmetic: 22.3 us -> 0 us
  matrix products: 12 us -> 0 us
    psum x1 -> x0, waiting for transfers between devices: 117 us -> none  [on_device(): lax.psum((edge_in_grad, edge_out_grad, node_in_grad, node_out_grad), ('gx...]
    ppermute x18 -> x0, starting transfers between devices: 37.4 us -> none  [the longest x9 25.8 us: extended(): lax.ppermute(lax.slice_in_dim(block, block.shape[dim] - width, None, axis...]
    pallas_call x0 -> x1, Pallas kernels: none -> 32.7 us  [on_device(): pl.pallas_call(functools.partial(kernel, sizes, group, rest), out_shape=(...]
    ppermute x18 -> x0, waiting for transfers between devices: 29.6 us -> none  [the longest x9 29.4 us: extended(): lax.ppermute(lax.slice_in_dim(block, 0, width, axis=dim), axis, backward)]
    dot_general x53 -> x0, matrix products: 12 us -> none  [the longest x19 5.76 us: outer_product(): lax.dot_general(left, right, (((0,), (0,)), ((), ())), preferred_element_...]
    and x10 -> x0, other arithmetic: 7.86 us -> none  [the longest x6 7.56 us: neighbour_valid(): (coords + offset[which] >= 0) & (coords + offset[which] < brick)]
    reduce_sum x4 -> x0, other arithmetic: 5.15 us -> none  [clip_all(): squares = sum((jnp.sum(single * single) for single in grads))]
    unnamed x26 -> x14, local copies, waits for them, and re-layouts: 1.63 us -> 6.76 us
  transfers between devices with their start and end apart: 19 -> 0, of which waited for: 11 -> 0; matrix products, arithmetic and copies ran while one was open for 2% -> 0% of each run, Pallas kernels for 0% -> 0%
where the time goes in v1:
time: 40.4 us; the launch traced here: 40.1 us
  Pallas kernels  32.7 us (81%)
  local copies, waits for them, and re-layouts  6.76 us (17%)
  between operations  0.65 us (2%)
    pallas_call x1, Pallas kernels, on_device(): pl.pallas_call(functools.partial(kernel, sizes, group, rest), out_shape=(...  32.7 us
    unnamed x14, local copies, waits for them, and re-layouts  6.76 us

profile of v1, /device:TPU:0, one launch (start us, length us, event | category | flops | bytes accessed | tf_op | source)
XLA Modules:
  0.0 40.1 jit_solution(6501931194487269715)
XLA Ops:
  0.6 32.7 %shard_map.136 = (bf16[512,128]{1,0:T(8,128)(2,1)}, bf16[2048,128]{1,0:T(8,128)(2,1)}, f32[384,128]{1,0:T(8,128)}, f32[128,128]{1,0:T(8,128)}, f32[256,128]{1,0:T(8,128)}, /*index=5*/f32[128,128]{1,0:T(8,128)}) custom-call(s32[4,3]{1,0:T(4,128)} %offs.1, bf16[512,128]{1,0:T(8,128)(2,1)} %bitcast.9, bf16[2048,128]{1,0:T(8,128)(2,1)} %bitcast.6, ...), custom_call_target="tpu_custom_call" | custom-call | tf_op jit(solution)/shard_map/pallas_call | solution.py:405
  33.3 1.6 %copy.21 = bf16[8,8,8,128]{3,2,1,0:T(8,128)(2,1)} copy(bf16[8,8,8,128]{3,2,1,0:T(8,128)(2,1)} %bitcast.8) | data formatting | bytes 262144
  34.9 0.0 copy-start
  34.9 1.9 %copy.22 = bf16[4,8,8,8,128]{4,3,2,1,0:T(8,128)(2,1)} copy(bf16[4,8,8,8,128]{4,3,2,1,0:T(8,128)(2,1)} %bitcast.7) | data formatting | bytes 1048576
  36.8 0.0 copy-done
  36.8 0.0 copy-start.3
  36.8 0.7 %copy.23 = f32[384,128]{1,0:T(8,128)} copy(f32[384,128]{1,0:T(8,128)S(1)} %copy-done) | data formatting | bytes 393216
  37.5 0.2 copy-done.3
  37.6 0.0 copy-start.1
  37.6 0.6 %copy.24 = f32[128,128]{1,0:T(8,128)} copy(f32[128,128]{1,0:T(8,128)S(1)} %copy-done.3) | data formatting | bytes 131072
  38.3 0.3 copy-done.1
  38.6 0.0 copy-start.2
  38.6 0.7 %copy.25 = f32[256,128]{1,0:T(8,128)} copy(f32[256,128]{1,0:T(8,128)S(1)} %copy-done.1) | data formatting | bytes 262144
  39.2 0.2 copy-done.2
  39.4 0.6 %copy.26 = f32[128,128]{1,0:T(8,128)} copy(f32[128,128]{1,0:T(8,128)S(1)} %copy-done.2) | data formatting | bytes 131072
Async XLA Ops:
  34.9 1.9 %copy-start = (f32[384,128]{1,0:T(8,128)S(1)}, f32[384,128]{1,0:T(8,128)}, u32[]{:S(2)}) copy-start(f32[384,128]{1,0:T(8,128)} %get-tuple-element.26) | copy-start | bytes 589828
  36.8 0.9 %copy-start.3 = (f32[128,128]{1,0:T(8,128)S(1)}, f32[128,128]{1,0:T(8,128)}, u32[]{:S(2)}) copy-start(f32[128,128]{1,0:T(8,128)} %get-tuple-element.27) | copy-start | bytes 196612
  37.6 0.9 %copy-start.1 = (f32[256,128]{1,0:T(8,128)S(1)}, f32[256,128]{1,0:T(8,128)}, u32[]{:S(2)}) copy-start(f32[256,128]{1,0:T(8,128)} %get-tuple-element.28) | copy-start | bytes 393220
  38.6 0.9 %copy-start.2 = (f32[128,128]{1,0:T(8,128)S(1)}, f32[128,128]{1,0:T(8,128)}, u32[]{:S(2)}) copy-start(f32[128,128]{1,0:T(8,128)} %get-tuple-element.29) | copy-start | bytes 196612

commit v2 on v1

--- a/solution.py
+++ b/solution.py
@@ -10,6 +10,9 @@
 
 F32 = jnp.float32
 BF16 = jnp.bfloat16
+VMEM_MAIN = 20 * 2**20
+VMEM_FINISH = 8 * 2**20
+FIN = pl.BlockSpec(memory_space=pl.ANY)
 AXES = ("gx", "gy", "gz")
 DIRS = [
     (dx, dy, dz)
@@ -53,10 +56,10 @@
 def kernel(
     sizes, group, rest,
     offs, node_ref, edge_ref, cop_ref, wei, weo, wni, wno, cot_ref,
-    o_node, o_edge, o_ei, o_eo, o_ni, o_no,
-    edges, egr, pad_a, pad_s, sl, hs, field, zs, field2,
+    o_node, o_edge, gn, ga, gb,
+    edges, egr, pad_a, pad_s, sl, field, zs, field2,
     rx, ry, rz, rxy, rxz, ryz, rxyz,
-    ng, eg, gn, ge, rbn, rbe, exn, exe,
+    ng, ea, eb, rbn, rba, rbb, exn, exa, exb,
     in_sem, out_sem, hs_sem, hr_sem, rs_s, rs_r, ex_s, ex_r, ag_s, ag_r,
 ):
     width = node_ref.shape[1]
@@ -176,7 +179,7 @@
         return ref.at[pl.ds(pl.multiple_of(rank * rows, 8), rows)]
 
     def rs_copy(w, j):
-        src, dst = (ng, rbn) if w == 0 else (eg, rbe)
+        src, dst = ((ng, rbn), (ea, rba), (eb, rbb))[w]
         to = lax.rem(me + j, members)
         rows = src.shape[0] // members
         return pltpu.make_async_remote_copy(
@@ -193,7 +196,7 @@
             rs_copy(w, j).start()
 
     def rs_finish(w):
-        src, dst = (ng, rbn) if w == 0 else (eg, rbe)
+        src, dst = ((ng, rbn), (ea, rba), (eb, rbb))[w]
         rows = src.shape[0] // members
         total = rows_at(src, me, rows)[...]
         for j in range(1, members):
@@ -208,7 +211,7 @@
         base += sizes[a]
 
     def ex_copy(w, e, j):
-        buf = exn if w == 0 else exe
+        buf = (exn, exa, exb)[w]
         a = rest[e]
         spot = buf.at[bases[e] + pos[a]]
         return pltpu.make_async_remote_copy(
@@ -221,13 +224,13 @@
         )
 
     def ex_start(w, e, total):
-        buf = exn if w == 0 else exe
+        buf = (exn, exa, exb)[w]
         buf[bases[e] + pos[rest[e]]] = total
         for j in range(1, sizes[rest[e]]):
             ex_copy(w, e, j).start()
 
     def ex_finish(w, e):
-        buf = exn if w == 0 else exe
+        buf = (exn, exa, exb)[w]
         for j in range(1, sizes[rest[e]]):
             ex_copy(w, e, j).wait_recv()
         total = buf[bases[e]]
@@ -243,7 +246,7 @@
         return total
 
     def ag_copy(w, j):
-        buf = gn if w == 0 else ge
+        buf = (gn, ga, gb)[w]
         spot = rows_at(buf, me, buf.shape[0] // members)
         return pltpu.make_async_remote_copy(
             src_ref=spot,
@@ -255,7 +258,7 @@
         )
 
     def ag_start(w, total):
-        buf = gn if w == 0 else ge
+        buf = (gn, ga, gb)[w]
         rows_at(buf, me, buf.shape[0] // members)[...] = total
         for j in range(1, members):
             ag_copy(w, j).start()
@@ -280,7 +283,6 @@
     picked = jnp.where(lane == row, picked, 0.0).astype(BF16)
     inverse = 1.0 / dot(picked, jnp.ones((brick, width), BF16))
     fetch.wait()
-    hiddens = []
     hidden_sum = None
     for k in range(kinds):
         o = [offs[k, axis] for axis in range(3)]
@@ -298,35 +300,36 @@
         valid = valid.reshape(count, width)
         sl[k] = jnp.where(valid, sigma + hidden * (1.0 - sigma), 0.0)
         hidden = jnp.where(valid, hidden, 0.0).astype(BF16)
-        hiddens.append(hidden)
         wide = hidden.astype(F32)
         hidden_sum = wide if hidden_sum is None else hidden_sum + wide
+    pl.semaphore_wait(barrier, waits)
+    halo_start(0, hidden_sum)
+
     w_out = weo[...]
-    local_sum = dot(
-        jnp.concatenate(hiddens, axis=1), jnp.concatenate([w_out] * kinds, axis=0)
-    )
-    pl.semaphore_wait(barrier, waits)
-    halo_start(0, local_sum)
-
-    hs[...] = hidden_sum.astype(BF16)
     cot = cot_ref[...]
     node_own = dot(node, wni[:width])
     upstream = dot_t(cot, wno[...])
-
-    summed = halo_finish(0)
+    twice = jnp.concatenate([w_out, w_out], axis=0)
+
+    joined = halo_finish(0)
+    high = joined.astype(BF16)
+    low = (joined - high.astype(F32)).astype(BF16)
+    summed = dot(jnp.concatenate([high, low], axis=1), twice)
     gathered = (summed * inverse).astype(BF16)
     pre = node_own + dot(gathered, wni[width:])
     sigma = 0.5 * jnp.tanh(0.5 * pre) + 0.5
     hidden = pre * sigma
     slope = (upstream * (sigma + hidden * (1.0 - sigma))).astype(BF16)
-    halo_start(1, dot_t(slope, wni[width:]) * inverse)
+    to_agg = dot_t(slope, wni[width:]) * inverse
+    halo_start(1, to_agg)
     ng[:width] = outer(node, slope)
     ng[width : 2 * width] = outer(gathered, slope)
-    ng[2 * width :] = outer(hidden.astype(BF16), cot)
+    ng[2 * width : 3 * width] = outer(hidden.astype(BF16), cot)
+    ng[3 * width :] = outer(high, to_agg.astype(BF16))
+    own = cot.astype(F32) + dot_t(slope, wni[:width])
+
+    arriving = halo_finish(1).astype(BF16)
     rs_start(0)
-    own = cot.astype(F32) + dot_t(slope, wni[:width])
-
-    arriving = halo_finish(1).astype(BF16)
     back = dot_t(arriving, w_out)
     slopes = []
     direct = None
@@ -344,44 +347,58 @@
     turned = turned.reshape(count, width).astype(BF16)
     direct = direct.astype(BF16)
     slope_all = jnp.concatenate(slopes, axis=0)
-    eg[:width] = outer(node, turned)
-    eg[width : 2 * width] = outer(node, direct)
-    eg[2 * width : 3 * width] = outer(edges[...], slope_all)
-    eg[3 * width :] = outer(hs[...], arriving)
+    ea[:width] = outer(node, turned)
+    ea[width:] = outer(node, direct)
     rs_start(1)
+    eb[...] = outer(edges[...], slope_all)
+    rs_start(2)
+    ex_start(0, 0, rs_finish(0))
     own = own + dot_t(turned, wei[:width]) + dot_t(direct, wei[width : 2 * width])
     halo_start(2, own)
-    ex_start(0, 0, rs_finish(0))
+    ex_start(1, 0, rs_finish(1))
+    ex_start(2, 0, rs_finish(2))
+    ag_start(0, ex_all(0))
+    ag_start(1, ex_all(1))
+    ag_start(2, ex_all(2))
     egr[...] = dot_t(slope_all, wei[2 * width :]).astype(BF16)
     store = pltpu.make_async_copy(egr, o_edge, out_sem)
     store.start()
-    ex_start(1, 0, rs_finish(1))
-    ag_start(0, ex_all(0))
     o_node[...] = halo_finish(2).astype(BF16)
-    ag_start(1, ex_all(1))
     ag_finish(0)
-    node_total = gn[...]
-    squares = jnp.sum(node_total * node_total, axis=0, keepdims=True)
     ag_finish(1)
-    edge_total = ge[...]
-    squares = squares + jnp.sum(edge_total * edge_total, axis=0, keepdims=True)
-    squares = jnp.sum(squares, axis=1, keepdims=True)
-    entries = (ge.shape[0] + gn.shape[0]) * width
-    factor = math.sqrt(entries) / jnp.sqrt(squares)
-    o_ei[...] = edge_total[: 3 * width] * factor
-    o_eo[...] = edge_total[3 * width :] * factor
-    o_ni[...] = node_total[: 2 * width] * factor
-    o_no[...] = node_total[2 * width :] * factor
+    ag_finish(2)
     store.wait()
     for a in range(3):
         halo_drain(a)
-    for w in range(2):
+    for w in range(3):
         for j in range(1, members):
             rs_copy(w, j).wait_send()
             ag_copy(w, j).wait_send()
         for e in range(len(rest)):
             for j in range(1, sizes[rest[e]]):
                 ex_copy(w, e, j).wait_send()
+
+
+def finish(node_in, edge_in, gn, ga, gb, o_node, o_edge, o_ei, o_eo, o_ni, o_no, sems):
+    width = gn.shape[1]
+    moves = [
+        pltpu.make_async_copy(edge_in, o_edge, sems.at[0]),
+        pltpu.make_async_copy(node_in, o_node, sems.at[1]),
+    ]
+    for move in moves:
+        move.start()
+    totals = [ref[...] for ref in (gn, ga, gb)]
+    squares = sum(jnp.sum(t * t, axis=0, keepdims=True) for t in totals)
+    squares = jnp.sum(squares, axis=1, keepdims=True)
+    entries = sum(t.shape[0] for t in totals) * width
+    factor = math.sqrt(entries) / jnp.sqrt(squares)
+    o_ei[: 2 * width] = totals[1] * factor
+    o_ei[2 * width :] = totals[2] * factor
+    o_ni[...] = totals[0][: 2 * width] * factor
+    o_no[...] = totals[0][2 * width : 3 * width] * factor
+    o_eo[...] = totals[0][3 * width :] * factor
+    for move in moves:
+        move.wait()
 
 
 def on_device(
@@ -391,9 +408,9 @@
     width = node_feat.shape[3]
     kinds = edge_feat.shape[0]
     count = brick**3
-    rows_n, rows_e = 3 * width, 4 * width
+    rows_n, rows_a, rows_b = 4 * width, 2 * width, width
     group, rest = ("gx", "gy"), ("gz",)
-    if math.gcd(rows_n, rows_e) % (8 * sizes["gx"] * sizes["gy"]) != 0:
+    if width % (8 * sizes["gx"] * sizes["gy"]) != 0:
         group, rest = ("gy",), ("gx", "gz")
     members = math.prod(sizes[a] for a in group)
     others = sum(sizes[a] for a in rest)
@@ -407,20 +424,18 @@
         out_shape=(
             jax.ShapeDtypeStruct((count, w), BF16),
             jax.ShapeDtypeStruct((kinds * count, w), BF16),
-            jax.ShapeDtypeStruct((3 * w, w), F32),
-            jax.ShapeDtypeStruct((w, w), F32),
-            jax.ShapeDtypeStruct((2 * w, w), F32),
-            jax.ShapeDtypeStruct((w, w), F32),
+            jax.ShapeDtypeStruct((rows_n, w), F32),
+            jax.ShapeDtypeStruct((rows_a, w), F32),
+            jax.ShapeDtypeStruct((rows_b, w), F32),
         ),
         in_specs=[smem, vmem, hbm, vmem, vmem, vmem, vmem, vmem, vmem],
-        out_specs=(vmem, hbm, vmem, vmem, vmem, vmem),
+        out_specs=(vmem, hbm, vmem, vmem, vmem),
         scratch_shapes=[
             pltpu.VMEM((kinds * count, w), BF16),
             pltpu.VMEM((kinds * count, w), BF16),
             pltpu.VMEM((b + 2, b + 2, b, w), F32),
             pltpu.VMEM((kinds, b + 2, b + 2, b, w), F32),
             pltpu.VMEM((kinds, count, w), F32),
-            pltpu.VMEM((count, w), BF16),
             pltpu.VMEM((3, b, b, b, w), F32),
             pltpu.VMEM((3, 2, b, b, 1, w), F32),
             pltpu.VMEM((3, b, b, b, w), F32),
@@ -431,26 +446,23 @@
             pltpu.VMEM((3, 4, b, 1, w), F32),
             pltpu.VMEM((3, 4, b, 1, w), F32),
             pltpu.VMEM((3, 8, 1, w), F32),
-            pltpu.VMEM((rows_n, w), F32),
-            pltpu.VMEM((rows_e, w), F32),
-            pltpu.VMEM((rows_n, w), F32),
-            pltpu.VMEM((rows_e, w), F32),
-            pltpu.VMEM((members, rows_n // members, w), F32),
-            pltpu.VMEM((members, rows_e // members, w), F32),
-            pltpu.VMEM((others, rows_n // members, w), F32),
-            pltpu.VMEM((others, rows_e // members, w), F32),
+            *[pltpu.VMEM((r, w), F32) for r in (rows_n, rows_a, rows_b)],
+            *[pltpu.VMEM((members, r // members, w), F32) for r in (rows_n, rows_a, rows_b)],
+            *[pltpu.VMEM((others, r // members, w), F32) for r in (rows_n, rows_a, rows_b)],
             dma,
             dma,
             dma((3, len(DIRS))),
             dma((3, len(DIRS))),
-            dma((2, members)),
-            dma((2, members)),
-            dma((2, others)),
-            dma((2, others)),
-            dma((2, members)),
-            dma((2, members)),
+            dma((3, members)),
+            dma((3, members)),
+            dma((3, others)),
+            dma((3, others)),
+            dma((3, members)),
+            dma((3, members)),
         ],
-        compiler_params=pltpu.CompilerParams(collective_id=0, has_side_effects=True),
+        compiler_params=pltpu.CompilerParams(
+            collective_id=0, has_side_effects=True, vmem_limit_bytes=VMEM_MAIN
+        ),
     )(
         offsets,
         node_feat.reshape(count, w),
@@ -462,7 +474,22 @@
         w_node_out,
         node_cot.reshape(count, w),
     )
-    return (outs[0].reshape(node_feat.shape), outs[1].reshape(edge_feat.shape)) + tuple(outs[2:])
+    done = pl.pallas_call(
+        finish,
+        out_shape=(
+            jax.ShapeDtypeStruct((count, w), BF16),
+            jax.ShapeDtypeStruct((kinds * count, w), BF16),
+            jax.ShapeDtypeStruct((3 * w, w), F32),
+            jax.ShapeDtypeStruct((w, w), F32),
+            jax.ShapeDtypeStruct((2 * w, w), F32),
+            jax.ShapeDtypeStruct((w, w), F32),
+        ),
+        in_specs=[FIN, FIN, vmem, vmem, vmem],
+        out_specs=(hbm, hbm, vmem, vmem, vmem, vmem),
+        scratch_shapes=[dma((2,))],
+        compiler_params=pltpu.CompilerParams(vmem_limit_bytes=VMEM_FINISH),
+    )(*outs)
+    return (done[0].reshape(node_feat.shape), done[1].reshape(edge_feat.shape)) + tuple(done[2:])
 
 
 def solution(mesh):

time: 40.4 us -> 44.6 us (1.10)
  Pallas kernels: 32.7 us -> 35.9 us
  local copies, waits for them, and re-layouts: 6.76 us -> 7.53 us
    pallas_call x0 -> x1, Pallas kernels: none -> 1.62 us  [on_device(): pl.pallas_call(finish, out_shape=(jax.ShapeDtypeStruct((count, w), BF16),...]
    pallas_call x1, Pallas kernels: 32.7 us -> 34.3 us  [on_device(): pl.pallas_call(functools.partial(kernel, sizes, group, rest), out_shape=(...]
    unnamed x14 -> x18, local copies, waits for them, and re-layouts: 6.76 us -> 7.53 us
where the time goes in v2:
time: 44.6 us; the launch traced here: 44.1 us
  Pallas kernels  35.9 us (80%)
  local copies, waits for them, and re-layouts  7.53 us (17%)
  between operations  0.66 us (1%)
    pallas_call x1, Pallas kernels, on_device(): pl.pallas_call(functools.partial(kernel, sizes, group, rest), out_shape=(...  34.3 us
    unnamed x18, local copies, waits for them, and re-layouts  7.53 us
    pallas_call x1, Pallas kernels, on_device(): pl.pallas_call(finish, out_shape=(jax.ShapeDtypeStruct((count, w), BF16),...  1.62 us

profile of v2, /device:TPU:0, one launch (start us, length us, event | category | flops | bytes accessed | tf_op | source)
XLA Modules:
  0.0 44.1 jit_solution(10958225573635253459)
XLA Ops:
  0.6 0.0 copy-start.8
  0.6 0.7 %copy-done.8 = s32[4,3]{1,0:T(4,128)S(1)} copy-done((s32[4,3]{1,0:T(4,128)S(1)}, s32[4,3]{1,0:T(4,128)}, u32[]{:S(2)}) %copy-start.8) | copy-done | bytes 72
  1.3 0.0 copy-start
  1.3 1.0 %copy-done = bf16[4,8,8,8,128]{4,3,2,1,0:T(8,128)(2,1)S(1)} copy-done((bf16[4,8,8,8,128]{4,3,2,1,0:T(8,128)(2,1)S(1)}, bf16[4,8,8,8,128]{4,3,2,1,0:T(8,128)(2,1)}, u32[]{:S(2)}) %copy-start) | copy-done | bytes 524312
  2.4 0.0 copy-start.1
  2.4 0.9 %copy-done.1 = bf16[8,8,8,128]{3,2,1,0:T(8,128)(2,1)S(1)} copy-done((bf16[8,8,8,128]{3,2,1,0:T(8,128)(2,1)S(1)}, bf16[8,8,8,128]{3,2,1,0:T(8,128)(2,1)}, u32[]{:S(2)}) %copy-start.1) | copy-done | bytes 131096
  3.3 0.0 copy-start.2
  3.3 0.9 %copy-done.2 = bf16[8,8,8,128]{3,2,1,0:T(8,128)(2,1)S(1)} copy-done((bf16[8,8,8,128]{3,2,1,0:T(8,128)(2,1)S(1)}, bf16[8,8,8,128]{3,2,1,0:T(8,128)(2,1)}, u32[]{:S(2)}) %copy-start.2) | copy-done | bytes 131096
  4.2 0.0 copy-start.3
  4.2 0.9 %copy-done.3 = bf16[384,128]{1,0:T(8,128)(2,1)S(1)} copy-done((bf16[384,128]{1,0:T(8,128)(2,1)S(1)}, bf16[384,128]{1,0:T(8,128)(2,1)}, u32[]{:S(2)}) %copy-start.3) | copy-done | bytes 98328
  5.1 0.0 copy-start.4
  5.1 0.8 %copy-done.4 = bf16[256,128]{1,0:T(8,128)(2,1)S(1)} copy-done((bf16[256,128]{1,0:T(8,128)(2,1)S(1)}, bf16[256,128]{1,0:T(8,128)(2,1)}, u32[]{:S(2)}) %copy-start.4) | copy-done | bytes 65560
  5.9 0.0 copy-start.5
  5.9 0.8 %copy-done.5 = s32[8,8,8]{2,1,0:T(8,128)S(1)} copy-done((s32[8,8,8]{2,1,0:T(8,128)S(1)}, s32[8,8,8]{2,1,0:T(8,128)}, u32[]{:S(2)}) %copy-start.5) | copy-done | bytes 2072
  6.7 0.0 copy-start.6
  6.7 0.8 %copy-done.6 = bf16[128,128]{1,0:T(8,128)(2,1)S(1)} copy-done((bf16[128,128]{1,0:T(8,128)(2,1)S(1)}, bf16[128,128]{1,0:T(8,128)(2,1)}, u32[]{:S(2)}) %copy-start.6) | copy-done | bytes 32792
  7.4 0.0 copy-start.7
  7.4 0.8 %copy-done.7 = bf16[128,128]{1,0:T(8,128)(2,1)S(1)} copy-done((bf16[128,128]{1,0:T(8,128)(2,1)S(1)}, bf16[128,128]{1,0:T(8,128)(2,1)}, u32[]{:S(2)}) %copy-start.7) | copy-done | bytes 32792
  8.2 34.3 %shard_map.136 = (bf16[512,128]{1,0:T(8,128)(2,1)S(1)}, bf16[2048,128]{1,0:T(8,128)(2,1)S(1)}, f32[512,128]{1,0:T(8,128)S(1)}, f32[256,128]{1,0:T(8,128)S(1)}, f32[128,128]{1,0:T(8,128)S(1)}) custom-call(s32[4,3]{1,0:T(4,128)S(1)} %copy-done.8, bf16[512,128]{1,0:T(8,128)(2,1)S(1)} %bitcast.7, bf16[2048,128]{1,0:T(8,128)(2,1)S(1)} %bitcast.6, ...), custom_call_target="tpu_custom_call" | custom-call | tf_op jit(solution)/shard_map/pallas_call | solution.py:422
  42.5 1.6 %shard_map.137 = (bf16[512,128]{1,0:T(8,128)(2,1)}, bf16[2048,128]{1,0:T(8,128)(2,1)}, f32[384,128]{1,0:T(8,128)}, f32[128,128]{1,0:T(8,128)}, f32[256,128]{1,0:T(8,128)}, /*index=5*/f32[128,128]{1,0:T(8,128)}) custom-call(bf16[512,128]{1,0:T(8,128)(2,1)S(1)} %get-tuple-element.17.node_in, bf16[2048,128]{1,0:T(8,128)(2,1)S(1)} %get-tuple-element.18.edge_in, ...), custom_call_target="tpu_custom_call" | custom-call | tf_op jit(solution)/shard_map/pallas_call | solution.py:477
Async XLA Ops:
  0.6 0.7 %copy-start.8 = (s32[4,3]{1,0:T(4,128)S(1)}, s32[4,3]{1,0:T(4,128)}, u32[]{:S(2)}) copy-start(s32[4,3]{1,0:T(4,128)} %offs.1) | copy-start | bytes 148
  1.3 1.0 %copy-start = (bf16[4,8,8,8,128]{4,3,2,1,0:T(8,128)(2,1)S(1)}, bf16[4,8,8,8,128]{4,3,2,1,0:T(8,128)(2,1)}, u32[]{:S(2)}) copy-start(bf16[4,8,8,8,128]{4,3,2,1,0:T(8,128)(2,1)} %param.10) | copy-start | bytes 1572868
  2.4 0.9 %copy-start.1 = (bf16[8,8,8,128]{3,2,1,0:T(8,128)(2,1)S(1)}, bf16[8,8,8,128]{3,2,1,0:T(8,128)(2,1)}, u32[]{:S(2)}) copy-start(bf16[8,8,8,128]{3,2,1,0:T(8,128)(2,1)} %param.9) | copy-start | bytes 393220
  3.3 0.9 %copy-start.2 = (bf16[8,8,8,128]{3,2,1,0:T(8,128)(2,1)S(1)}, bf16[8,8,8,128]{3,2,1,0:T(8,128)(2,1)}, u32[]{:S(2)}) copy-start(bf16[8,8,8,128]{3,2,1,0:T(8,128)(2,1)} %param.17) | copy-start | bytes 393220
  4.2 0.9 %copy-start.3 = (bf16[384,128]{1,0:T(8,128)(2,1)S(1)}, bf16[384,128]{1,0:T(8,128)(2,1)}, u32[]{:S(2)}) copy-start(bf16[384,128]{1,0:T(8,128)(2,1)} %wei.1) | copy-start | bytes 294916
  5.1 0.8 %copy-start.4 = (bf16[256,128]{1,0:T(8,128)(2,1)S(1)}, bf16[256,128]{1,0:T(8,128)(2,1)}, u32[]{:S(2)}) copy-start(bf16[256,128]{1,0:T(8,128)(2,1)} %wni.1) | copy-start | bytes 196612
  5.9 0.8 %copy-start.5 = (s32[8,8,8]{2,1,0:T(8,128)S(1)}, s32[8,8,8]{2,1,0:T(8,128)}, u32[]{:S(2)}) copy-start(s32[8,8,8]{2,1,0:T(8,128)} %param.11) | copy-start | bytes 6148
  6.7 0.8 %copy-start.6 = (bf16[128,128]{1,0:T(8,128)(2,1)S(1)}, bf16[128,128]{1,0:T(8,128)(2,1)}, u32[]{:S(2)}) copy-start(bf16[128,128]{1,0:T(8,128)(2,1)} %weo.1) | copy-start | bytes 98308
  7.4 0.8 %copy-start.7 = (bf16[128,128]{1,0:T(8,128)(2,1)S(1)}, bf16[128,128]{1,0:T(8,128)(2,1)}, u32[]{:S(2)}) copy-start(bf16[128,128]{1,0:T(8,128)(2,1)} %wno.1) | copy-start | bytes 98308

commit v3 on v2

--- a/solution.py
+++ b/solution.py
@@ -55,9 +55,9 @@
 
 def kernel(
     sizes, group, rest,
-    offs, node_ref, edge_ref, cop_ref, wei, weo, wni, wno, cot_ref,
+    offs_hbm, node_hbm, edge_hbm, cop_hbm, wei_hbm, weo_hbm, wni_hbm, wno_hbm, cot_hbm,
     o_node, o_edge, gn, ga, gb,
-    edges, egr, pad_a, pad_s, sl, field, zs, field2,
+    offs, node_ref, edges, cop_ref, wei, weo, wni, wno, cot_ref, egr, pad_a, pad_s, sl, field, zs, field2,
     rx, ry, rz, rxy, rxz, ryz, rxyz,
     ng, ea, eb, rbn, rba, rbb, exn, exa, exb,
     in_sem, out_sem, hs_sem, hr_sem, rs_s, rs_r, ex_s, ex_r, ag_s, ag_r,
@@ -71,8 +71,17 @@
     pos = {a: lax.axis_index(a) for a in AXES}
     recv = {"x": rx, "y": ry, "z": rz, "xy": rxy, "xz": rxz, "yz": ryz, "xyz": rxyz}
 
-    fetch = pltpu.make_async_copy(edge_ref, edges, in_sem)
-    fetch.start()
+    fetches = [
+        pltpu.make_async_copy(src, dst, in_sem.at[i])
+        for i, (src, dst) in enumerate(
+            (
+                (node_hbm, node_ref), (wei_hbm, wei), (edge_hbm, edges), (cop_hbm, cop_ref),
+                (weo_hbm, weo), (wni_hbm, wni), (wno_hbm, wno), (cot_hbm, cot_ref), (offs_hbm, offs),
+            )
+        )
+    ]
+    for fetch in fetches:
+        fetch.start()
 
     def exists(d, sign):
         ok = None
@@ -267,9 +276,11 @@
         for j in range(1, members):
             ag_copy(w, j).wait_recv()
 
-    node = node_ref[...]
     pad_a[...] = jnp.zeros_like(pad_a)
     pad_s[...] = jnp.zeros_like(pad_s)
+    for fetch in fetches:
+        fetch.wait()
+    node = node_ref[...]
     pad_a[1 : brick + 1, 1 : brick + 1] = dot(node, wei[:width]).reshape(cube)
     received = dot(node, wei[width : 2 * width])
     coords = [lax.broadcasted_iota(jnp.int32, cube, axis) for axis in range(3)]
@@ -282,7 +293,6 @@
     row = lax.broadcasted_iota(jnp.int32, (count, brick), 0) % brick
     picked = jnp.where(lane == row, picked, 0.0).astype(BF16)
     inverse = 1.0 / dot(picked, jnp.ones((brick, width), BF16))
-    fetch.wait()
     hidden_sum = None
     for k in range(kinds):
         o = [offs[k, axis] for axis in range(3)]
@@ -415,8 +425,8 @@
     members = math.prod(sizes[a] for a in group)
     others = sum(sizes[a] for a in rest)
     vmem = pl.BlockSpec(memory_space=pltpu.VMEM)
-    smem = pl.BlockSpec(memory_space=pltpu.SMEM)
     hbm = pl.BlockSpec(memory_space=pl.ANY)
+    far = pl.BlockSpec(memory_space=pltpu.HBM)
     dma = pltpu.SemaphoreType.DMA
     b, w = brick, width
     outs = pl.pallas_call(
@@ -428,10 +438,18 @@
             jax.ShapeDtypeStruct((rows_a, w), F32),
             jax.ShapeDtypeStruct((rows_b, w), F32),
         ),
-        in_specs=[smem, vmem, hbm, vmem, vmem, vmem, vmem, vmem, vmem],
+        in_specs=[far] * 9,
         out_specs=(vmem, hbm, vmem, vmem, vmem),
         scratch_shapes=[
+            pltpu.SMEM(offsets.shape, jnp.int32),
+            pltpu.VMEM((count, w), BF16),
             pltpu.VMEM((kinds * count, w), BF16),
+            pltpu.VMEM((b * b, b), jnp.int32),
+            pltpu.VMEM((3 * w, w), BF16),
+            pltpu.VMEM((w, w), BF16),
+            pltpu.VMEM((2 * w, w), BF16),
+            pltpu.VMEM((w, w), BF16),
+            pltpu.VMEM((count, w), BF16),
             pltpu.VMEM((kinds * count, w), BF16),
             pltpu.VMEM((b + 2, b + 2, b, w), F32),
             pltpu.VMEM((kinds, b + 2, b + 2, b, w), F32),
@@ -449,7 +467,7 @@
             *[pltpu.VMEM((r, w), F32) for r in (rows_n, rows_a, rows_b)],
             *[pltpu.VMEM((members, r // members, w), F32) for r in (rows_n, rows_a, rows_b)],
             *[pltpu.VMEM((others, r // members, w), F32) for r in (rows_n, rows_a, rows_b)],
-            dma,
+            dma((9,)),
             dma,
             dma((3, len(DIRS))),
             dma((3, len(DIRS))),
@@ -464,15 +482,20 @@
             collective_id=0, has_side_effects=True, vmem_limit_bytes=VMEM_MAIN
         ),
     )(
-        offsets,
-        node_feat.reshape(count, w),
-        edge_feat.reshape(kinds * count, w),
-        copies.reshape(b * b, b),
-        w_edge_in,
-        w_edge_out,
-        w_node_in,
-        w_node_out,
-        node_cot.reshape(count, w),
+        pltpu.with_memory_space_constraint(offsets, pltpu.HBM),
+        *[
+            pltpu.with_memory_space_constraint(array, pltpu.HBM)
+            for array in (
+                node_feat.reshape(count, w),
+                edge_feat.reshape(kinds * count, w),
+                copies.reshape(b * b, b),
+                w_edge_in,
+                w_edge_out,
+                w_node_in,
+                w_node_out,
+                node_cot.reshape(count, w),
+            )
+        ],
     )
     done = pl.pallas_call(
         finish,

time: 44.6 us -> 36.2 us (0.81)
  local copies, waits for them, and re-layouts: 7.53 us -> 0 us
  Pallas kernels: 35.9 us -> 35.4 us
    unnamed x18 -> x0, local copies, waits for them, and re-layouts: 7.53 us -> none
    pallas_call x1, Pallas kernels: 34.3 us -> 33.8 us  [on_device(): pl.pallas_call(functools.partial(kernel, sizes, group, rest), out_shape=(...]
where the time goes in v3:
time: 36.2 us; the launch traced here: 36 us
  Pallas kernels  35.4 us (98%)
  between operations  0.64 us (2%)
    pallas_call x1, Pallas kernels, on_device(): pl.pallas_call(functools.partial(kernel, sizes, group, rest), out_shape=(...  33.8 us
    pallas_call x1, Pallas kernels, on_device(): pl.pallas_call(finish, out_shape=(jax.ShapeDtypeStruct((count, w), BF16),...  1.62 us

profile of v3, /device:TPU:0, one launch (start us, length us, event | category | flops | bytes accessed | tf_op | source)
XLA Modules:
  0.0 36.0 jit_solution(13400716564244039541)
XLA Ops:
  0.6 33.8 %shard_map.136 = (bf16[512,128]{1,0:T(8,128)(2,1)S(1)}, bf16[2048,128]{1,0:T(8,128)(2,1)S(1)}, f32[512,128]{1,0:T(8,128)S(1)}, f32[256,128]{1,0:T(8,128)S(1)}, f32[128,128]{1,0:T(8,128)S(1)}) custom-call(s32[4,3]{1,0:T(4,128)} %offs_hbm.1, bf16[512,128]{1,0:T(8,128)(2,1)} %bitcast.7, bf16[2048,128]{1,0:T(8,128)(2,1)} %bitcast.6, s32[64,8]{1,0:T(8,128)} %bitcast.9, ...), custom_call_target="tpu_custom_call" | custom-call | tf_op jit(solution)/shard_map/pallas_call | solution.py:432
  34.4 1.6 %shard_map.137 = (bf16[512,128]{1,0:T(8,128)(2,1)}, bf16[2048,128]{1,0:T(8,128)(2,1)}, f32[384,128]{1,0:T(8,128)}, f32[128,128]{1,0:T(8,128)}, f32[256,128]{1,0:T(8,128)}, /*index=5*/f32[128,128]{1,0:T(8,128)}) custom-call(bf16[512,128]{1,0:T(8,128)(2,1)S(1)} %get-tuple-element.17.node_in, bf16[2048,128]{1,0:T(8,128)(2,1)S(1)} %get-tuple-element.18.edge_in, ...), custom_call_target="tpu_custom_call" | custom-call | tf_op jit(solution)/shard_map/pallas_call | solution.py:500

commit v4 on v3

--- a/solution.py
+++ b/solution.py
@@ -336,10 +336,10 @@
     ng[width : 2 * width] = outer(gathered, slope)
     ng[2 * width : 3 * width] = outer(hidden.astype(BF16), cot)
     ng[3 * width :] = outer(high, to_agg.astype(BF16))
+    rs_start(0)
     own = cot.astype(F32) + dot_t(slope, wni[:width])
 
     arriving = halo_finish(1).astype(BF16)
-    rs_start(0)
     back = dot_t(arriving, w_out)
     slopes = []
     direct = None
@@ -364,9 +364,9 @@
     rs_start(2)
     ex_start(0, 0, rs_finish(0))
     own = own + dot_t(turned, wei[:width]) + dot_t(direct, wei[width : 2 * width])
-    halo_start(2, own)
     ex_start(1, 0, rs_finish(1))
     ex_start(2, 0, rs_finish(2))
+    halo_start(2, own)
     ag_start(0, ex_all(0))
     ag_start(1, ex_all(1))
     ag_start(2, ex_all(2))

time: 36.2 us -> 33.2 us (0.917)
  Pallas kernels: 35.4 us -> 32.4 us
    pallas_call x1, Pallas kernels: 33.8 us -> 30.8 us  [on_device(): pl.pallas_call(functools.partial(kernel, sizes, group, rest), out_shape=(...]
where the time goes in v4:
time: 33.2 us; the launch traced here: 33.1 us
  Pallas kernels  32.4 us (98%)
  between operations  0.64 us (2%)
    pallas_call x1, Pallas kernels, on_device(): pl.pallas_call(functools.partial(kernel, sizes, group, rest), out_shape=(...  30.8 us
    pallas_call x1, Pallas kernels, on_device(): pl.pallas_call(finish, out_shape=(jax.ShapeDtypeStruct((count, w), BF16),...  1.62 us

profile of v4, /device:TPU:0, one launch (start us, length us, event | category | flops | bytes accessed | tf_op | source)
XLA Modules:
  0.0 33.1 jit_solution(11337578925922705967)
XLA Ops:
  0.6 30.8 %shard_map.136 = (bf16[512,128]{1,0:T(8,128)(2,1)S(1)}, bf16[2048,128]{1,0:T(8,128)(2,1)S(1)}, f32[512,128]{1,0:T(8,128)S(1)}, f32[256,128]{1,0:T(8,128)S(1)}, f32[128,128]{1,0:T(8,128)S(1)}) custom-call(s32[4,3]{1,0:T(4,128)} %offs_hbm.1, bf16[512,128]{1,0:T(8,128)(2,1)} %bitcast.7, bf16[2048,128]{1,0:T(8,128)(2,1)} %bitcast.6, s32[64,8]{1,0:T(8,128)} %bitcast.9, ...), custom_call_target="tpu_custom_call" | custom-call | tf_op jit(solution)/shard_map/pallas_call | solution.py:432
  31.5 1.6 %shard_map.137 = (bf16[512,128]{1,0:T(8,128)(2,1)}, bf16[2048,128]{1,0:T(8,128)(2,1)}, f32[384,128]{1,0:T(8,128)}, f32[128,128]{1,0:T(8,128)}, f32[256,128]{1,0:T(8,128)}, /*index=5*/f32[128,128]{1,0:T(8,128)}) custom-call(bf16[512,128]{1,0:T(8,128)(2,1)S(1)} %get-tuple-element.17.node_in, bf16[2048,128]{1,0:T(8,128)(2,1)S(1)} %get-tuple-element.18.edge_in, ...), custom_call_target="tpu_custom_call" | custom-call | tf_op jit(solution)/shard_map/pallas_call | solution.py:500
